TPU v7x, 256 devices: a whole 4x4x8 slice. The times are simulated.
256 devices in a mesh: row: 8 (over x, z_hi), col: 32 (over z_lo, y, core).
Axes of the slice: x: 4, y: 4, z: 8 (z_hi: 2, z_lo: 4; z = z_hi * 4 + z_lo), core: 2. Of those that a mesh axis runs over, the one named last changes fastest.
Arguments:
- adj_tiles: bfloat16 [8, 32, 160, 128, 128], P('row', 'col'), may hold values from -0.125 to 0.125
- tile_row: int32 [8, 32, 160], P('row', 'col'), may hold values from 0 to 31, as said below
- tile_col: int32 [8, 32, 160], P('row', 'col'), may hold values from 0 to 7
- tile_count: int32 [8, 32], P('row', 'col'), may hold values from 0 to 160, as said below
- node_feats: bfloat16 [32768, 512], P(('row', 'col')), may hold values from -24 to 24
- pre_act: bfloat16 [32768, 512], P(('col', 'row')), may hold values from -24 to 24
- out_grad: bfloat16 [32768, 512], P(('row', 'col')), may hold values from -0.08984375 to 0.08984375
- second_weight: bfloat16 [512, 512], replicated, may hold values from -0.25 to 0.25
Outputs:
- grad_first: float32 [512, 512], replicated
- grad_second: float32 [512, 512], replicated
Inputs may be any that keep to these rules, and one draw needn't show every extreme that they name: Within one block the slots name distinct tile positions (tile_row, tile_col). `tile_count`: blocks whose node columns meet their node rows hold 80 to 160 live slots, one of them exactly 160; every other block holds at most 8.
All inputs are finite; a program needn't handle non-finite values.
Results may differ from a plain program's by a relative error of at most 0.024.
Values may be sent and summed in bfloat16 or wider, within the bound.
A program may use at most 128 MiB of HBM per device.

v0:
```python
import jax
import jax.numpy as jnp
from jax import lax
from jax.sharding import PartitionSpec as P


def block_product(local_tiles, in_index, out_index, live_count, panel, out_tiles, transpose):
    slot_count = local_tiles.shape[0]
    tile_size = local_tiles.shape[1]
    panel_width = panel.shape[1]
    blocked = panel.reshape(-1, tile_size, panel_width)
    group_size = min(32, slot_count)
    turn_count = (live_count + group_size - 1) // group_size
    pattern = "bij,biw->bjw" if transpose else "bij,bjw->biw"

    def visit_group(turn_index, running):
        opening = turn_index * group_size
        offset = jnp.minimum(opening, slot_count - group_size)
        picked = lax.dynamic_slice_in_dim(local_tiles, offset, group_size, 0)
        source = lax.dynamic_slice_in_dim(in_index, offset, group_size, 0)
        target = lax.dynamic_slice_in_dim(out_index, offset, group_size, 0)
        gathered = blocked[source]
        products = jnp.einsum(pattern, picked, gathered, preferred_element_type=jnp.float32)
        placed = offset + jnp.arange(group_size, dtype=jnp.int32)
        usable = (placed >= opening) & (placed < live_count)
        select = (
            (target[None, :] == jnp.arange(out_tiles, dtype=jnp.int32)[:, None]) & usable[None, :]
        ).astype(jnp.float32)
        return running + jnp.einsum("ob,bjw->ojw", select, products)

    initial = jnp.zeros((out_tiles, tile_size, panel_width), jnp.float32)
    running = lax.fori_loop(0, turn_count, visit_group, initial)
    return running.reshape(out_tiles * tile_size, panel_width)


def shards(adj_tiles, tile_row, tile_col, tile_count, node_feats, pre_act, out_grad, second_weight):
    local_tiles = adj_tiles[0, 0]
    row_index = tile_row[0, 0]
    col_index = tile_col[0, 0]
    live_count = tile_count[0, 0]
    tile_size = local_tiles.shape[1]
    row_tiles = out_grad.shape[0] * lax.axis_size("col") // tile_size
    col_tiles = pre_act.shape[0] * lax.axis_size("row") // tile_size
    cot_block = lax.all_gather(out_grad, "col", axis=0, tiled=True)
    back_part = block_product(
        local_tiles, row_index, col_index, live_count, cot_block, col_tiles, True
    )
    back_local = lax.psum_scatter(
        back_part.astype(jnp.bfloat16), "row", scatter_dimension=0, tiled=True
    )
    hidden_act = jnp.maximum(pre_act, 0)
    second_part = lax.dot_general(
        hidden_act, back_local, (((0,), (0,)), ((), ())), preferred_element_type=jnp.float32
    )
    grad_second = lax.psum(second_part, ("row", "col"))
    hidden_grad = lax.dot_general(
        back_local, second_weight, (((1,), (1,)), ((), ())), preferred_element_type=jnp.float32
    )
    pre_grad = jnp.where(pre_act > 0, hidden_grad, 0.0).astype(jnp.bfloat16)
    grad_block = lax.all_gather(pre_grad, "row", axis=0, tiled=True)
    fwd_part = block_product(
        local_tiles, col_index, row_index, live_count, grad_block, row_tiles, False
    )
    fwd_local = lax.psum_scatter(
        fwd_part.astype(jnp.bfloat16), "col", scatter_dimension=0, tiled=True
    )
    first_part = lax.dot_general(
        node_feats, fwd_local, (((0,), (0,)), ((), ())), preferred_element_type=jnp.float32
    )
    grad_first = lax.psum(first_part, ("row", "col"))
    return (grad_first, grad_second)


def solution(mesh):
    in_specs = (
        P("row", "col", None, None, None),
        P("row", "col", None),
        P("row", "col", None),
        P("row", "col"),
        P(("row", "col"), None),
        P(("col", "row"), None),
        P(("row", "col"), None),
        P(),
    )
    out_specs = (P(), P())
    return jax.shard_map(shards, mesh=mesh, in_specs=in_specs, out_specs=out_specs, check_vma=False)
```

profile of v0, /device:TPU:1, one launch (start us, length us, event | category | flops | bytes accessed | tf_op | source)
XLA Modules:
  0.0 811.1 jit_solution(2811901382788987889)
XLA Ops:
  7.2 0.7 all-gather.3.cloned.1.call-update
  8.6 68.4 %all-gather.3.cloned.1.call-done = bf16[4096,512]{1,0:T(8,128)(2,1)} async-done(((bf16[128,512]{1,0:T(8,128)(2,1)}), bf16[4096,512]{1,0:T(8,128)(2,1)}) %all-gather.3.cloned.1.call-update) | async-done | bytes 4194320 | tf_op jit(solution)/shard_map/all_gather | solution.py:44
  77.0 0.2 broadcast_in_dim.23
  77.3 51.6 %while.20 = (s32[]{:T(128)}, f32[8,128,512]{2,0,1:T(8,128)S(1)}, s32[]{:T(128)}, s32[160]{0:T(256)}, s32[]{:T(128)}, /*index=5*/bf16[160,128,128]{2,1,0:T(8,128)...) while((s32[]{:T(128)}, f32[8,128,512]{2,0,1:T(8,128)S(1)}, ...), condition=%wide.region_1.2_spmd, body=%wide.region_0.1_spmd.sunk | while | flops 570951424 | bytes 26222252 | solution.py:32
  77.3 0.8 compare_select_fusion.4
  78.1 5.0 gather_fusion
  83.1 3.8 fusion.54
  86.9 0.1 dynamic_slice.32
  87.0 0.7 compare_and_fusion.4
  87.6 2.5 fusion.55
  90.2 0.8 compare_select_fusion.4
  91.0 5.0 gather_fusion
  95.9 3.8 fusion.54
  99.8 0.1 dynamic_slice.32
  99.9 0.7 compare_and_fusion.4
  100.5 2.5 fusion.55
  103.1 0.8 compare_select_fusion.4
  103.8 5.0 gather_fusion
  108.8 3.8 fusion.54
  112.7 0.1 dynamic_slice.32
  112.7 0.7 compare_and_fusion.4
  113.4 2.5 fusion.55
  116.0 0.8 compare_select_fusion.4
  116.7 5.0 gather_fusion
  121.7 3.8 fusion.54
  125.6 0.1 dynamic_slice.32
  125.6 0.7 compare_and_fusion.4
  126.3 2.5 fusion.55
  128.9 2.1 copy.27
  131.0 95.5 %reduce-scatter.3.cloned.1.call-done = bf16[128,512]{1,0:T(8,128)(2,1)} async-done(((bf16[1024,512]{1,0:T(8,128)(2,1)}), bf16[128,512]{1,0:T(8,128)(2,1)}) %reduce-scatter.3.cloned.1.call-update) | async-done | bytes 131088 | tf_op jit(solution)/shard_map/reduce_scatter | solution.py:48
  226.6 1.9 fusion.26
  228.5 59.6 %all-gather.5.cloned.1.call-done = bf16[1024,512]{1,0:T(8,128)(2,1)} async-done(((bf16[128,512]{1,0:T(8,128)(2,1)}), bf16[1024,512]{1,0:T(8,128)(2,1)}) %all-gather.5.cloned.1.call-update) | async-done | bytes 1048592 | tf_op jit(solution)/shard_map/all_gather | solution.py:60
  288.1 4.3 broadcast_in_dim.22
  292.5 70.3 %while.21 = (s32[]{:T(128)}, f32[32,128,512]{2,0,1:T(8,128)}, s32[]{:T(128)}, s32[160]{0:T(256)S(1)}, s32[]{:T(128)}, /*index=5*/bf16[160,128,128]{2,1,0:T(8,128...) while((s32[]{:T(128)}, f32[32,128,512]{2,0,1:T(8,128)}, ...), condition=%wide.region_4.5_spmd, body=%wide.region_3.4_spmd.sunk | while | flops 673189120 | bytes 38802576 | solution.py:32
  292.5 0.1 compare_select_fusion.5
  292.6 2.8 gather_fusion.1
  295.4 3.7 fusion.60
  299.1 0.1 dynamic_slice.35
  299.2 0.7 compare_and_fusion.5
  299.8 10.2 %fusion.61 = f32[32,128,512]{2,0,1:T(8,128)} fusion(f32[32,128,512]{2,0,1:T(8,128)} %get-tuple-element.281, bf16[32,128,512]{2,1,0:T(8,128)(2,1)S(1)} %fusion.60, s32[32]{0:T(128)S(1)} %dynamic_slice.35, pred[32]{0:T(512)(128)(4,1)S(1)} %compare_and_fusion.5), kind=kOutput, calls=%fused_computation.18.clone.1 | convolution fusion | flops 136316928 | bytes 20971680 | tf_op jit(solution)/shard_map/while/body/ob,bjw->ojw/dot_general | solution.py:29
  310.1 0.1 compare_select_fusion.5
  310.1 2.8 gather_fusion.1
  312.9 3.7 fusion.60
  316.7 0.1 dynamic_slice.35
  316.8 0.7 compare_and_fusion.5
  317.4 10.2 %fusion.61 = f32[32,128,512]{2,0,1:T(8,128)} fusion(f32[32,128,512]{2,0,1:T(8,128)} %get-tuple-element.281, bf16[32,128,512]{2,1,0:T(8,128)(2,1)S(1)} %fusion.60, s32[32]{0:T(128)S(1)} %dynamic_slice.35, pred[32]{0:T(512)(128)(4,1)S(1)} %compare_and_fusion.5), kind=kOutput, calls=%fused_computation.18.clone.1 | convolution fusion | flops 136316928 | bytes 20971680 | tf_op jit(solution)/shard_map/while/body/ob,bjw->ojw/dot_general | solution.py:29
  327.7 2.8 gather_fusion.1
  330.5 3.7 fusion.60
  334.2 0.1 dynamic_slice.35
  334.3 0.7 compare_and_fusion.5
  335.0 10.2 %fusion.61 = f32[32,128,512]{2,0,1:T(8,128)} fusion(f32[32,128,512]{2,0,1:T(8,128)} %get-tuple-element.281, bf16[32,128,512]{2,1,0:T(8,128)(2,1)S(1)} %fusion.60, s32[32]{0:T(128)S(1)} %dynamic_slice.35, pred[32]{0:T(512)(128)(4,1)S(1)} %compare_and_fusion.5), kind=kOutput, calls=%fused_computation.18.clone.1 | convolution fusion | flops 136316928 | bytes 20971680 | tf_op jit(solution)/shard_map/while/body/ob,bjw->ojw/dot_general | solution.py:29
  345.3 2.8 gather_fusion.1
  348.1 3.7 fusion.60
  351.8 0.1 dynamic_slice.35
  351.9 0.7 compare_and_fusion.5
  352.5 10.2 %fusion.61 = f32[32,128,512]{2,0,1:T(8,128)} fusion(f32[32,128,512]{2,0,1:T(8,128)} %get-tuple-element.281, bf16[32,128,512]{2,1,0:T(8,128)(2,1)S(1)} %fusion.60, s32[32]{0:T(128)S(1)} %dynamic_slice.35, pred[32]{0:T(512)(128)(4,1)S(1)} %compare_and_fusion.5), kind=kOutput, calls=%fused_computation.18.clone.1 | convolution fusion | flops 136316928 | bytes 20971680 | tf_op jit(solution)/shard_map/while/body/ob,bjw->ojw/dot_general | solution.py:29
  362.8 9.8 %copy.26 = bf16[32,128,512]{2,1,0:T(8,128)(2,1)} copy(f32[32,128,512]{2,0,1:T(8,128)} %get-tuple-element.89) | data formatting | bytes 12582912 | tf_op jit(solution)/shard_map/while | solution.py:32
  372.6 0.8 copy-done.3
  373.5 1.3 fusion.27
  374.8 156.4 %reduce-scatter.5.cloned.1.call-done = bf16[128,512]{1,0:T(8,128)(2,1)} async-done(((bf16[4096,512]{1,0:T(8,128)(2,1)}), bf16[128,512]{1,0:T(8,128)(2,1)}) %reduce-scatter.5.cloned.1.call-update) | async-done | bytes 131088 | tf_op jit(solution)/shard_map/reduce_scatter | solution.py:64
  531.2 2.2 convolution_bitcast_fusion
  533.4 266.4 %all-reduce.3.cloned.1.call-done = (f32[512,512]{0,1:T(8,128)}, f32[512,512]{1,0:T(8,128)}) async-done(((f32[512,512]{0,1:T(8,128)}, f32[512,512]{1,0:T(8,128)}), (f32[512,512]{0,1:T(8,128)}, f32[512,512]{1,0:T(8,128)})) %all-reduce.3.cloned.1.call-update) | async-done | bytes 2097168 | tf_op jit(solution)/shard_map/psum | solution.py:70
  799.8 2.5 copy.13
  802.3 2.3 copy.47
  (40 shorter events, 0.5 us)
Async XLA Ops:
  7.2 219.4 %copy-start = (bf16[512,512]{1,0:T(8,128)(2,1)S(1)}, bf16[512,512]{1,0:T(8,128)(2,1)}, u32[]{:S(2)}) copy-start(bf16[512,512]{1,0:T(8,128)(2,1)} %param.19) | copy-start | bytes 1572868
  7.2 69.8 %all-gather.3.cloned.1.call-start = ((), (), s32[]{:S(2)}) async-start(), calls=%async_computation.2 | async-start | bytes 4325376 | tf_op jit(solution)/shard_map/all_gather | solution.py:44
  7.9 218.6 %reduce-scatter.3.cloned.1.call-start = ((), (), s32[]{:S(2)}) async-start(), calls=%async_computation.3 | async-start | bytes 1179648 | tf_op jit(solution)/shard_map/reduce_scatter | solution.py:48
  83.1 3.8 copy-start.5
  95.9 3.8 copy-start.5
  108.8 3.8 copy-start.5
  121.7 3.8 copy-start.5
  128.8 97.7 %copy-start.2 = (bf16[128,512]{1,0:T(8,128)(2,1)S(1)}, bf16[128,512]{1,0:T(8,128)(2,1)}, u32[]{:S(2)}) copy-start(bf16[128,512]{1,0:T(8,128)(2,1)} %param.17) | copy-start | bytes 393220
  131.0 157.2 %all-gather.5.cloned.1.call-start = ((), (), s32[]{:S(2)}) async-start(), calls=%async_computation.4 | async-start | bytes 1179648 | tf_op jit(solution)/shard_map/all_gather | solution.py:60
  228.4 302.7 %reduce-scatter.5.cloned.1.call-start = ((), (), s32[]{:S(2)}) async-start(), calls=%async_computation.5 | async-start | bytes 4325376 | tf_op jit(solution)/shard_map/reduce_scatter | solution.py:64
  288.1 4.3 copy-start.1
  288.1 4.3 copy-start.6
  288.1 4.3 copy-start.7
  372.6 0.9 copy-start.3
  372.6 158.6 %copy-start.4 = (bf16[128,512]{1,0:T(8,128)(2,1)S(1)}, bf16[128,512]{1,0:T(8,128)(2,1)}, u32[]{:S(2)}) copy-start(bf16[128,512]{1,0:T(8,128)(2,1)} %param.16) | copy-start | bytes 393220
  372.6 427.2 %all-reduce.3.cloned.1.call-start = ((), (), s32[]{:S(2)}) async-start(), calls=%async_computation.6 | async-start | bytes 4194304 | tf_op jit(solution)/shard_map/psum | solution.py:70
Sparse Core Ops, SparseCore 0:
  9.9 67.1 all-gather.2
  131.1 95.4 reduce-scatter.2
  230.1 58.0 all-gather.4
  372.7 158.3 reduce-scatter.4
  538.0 261.6 all-reduce.2
where the time goes:
time: 813 us; the launch traced here: 811 us
  waiting for transfers between devices  647 us (80%)
  matrix products  86.6 us (11%)
  local copies, waits for them, and re-layouts  53.8 us (7%)
  between operations  14.5 us (2%)
  other arithmetic  8.61 us (1%)
    psum x1, waiting for transfers between devices, shards(): grad_first = lax.psum(first_part, ('row', 'col'))  266 us
    reduce_scatter x1, waiting for transfers between devices, shards(): lax.psum_scatter(fwd_part.astype(jnp.bfloat16), 'col', scatter_dimension=...  156 us
    reduce_scatter x1, waiting for transfers between devices, shards(): lax.psum_scatter(back_part.astype(jnp.bfloat16), 'row', scatter_dimension...  95.5 us
    all_gather x1, waiting for transfers between devices, shards(): cot_block = lax.all_gather(out_grad, 'col', axis=0, tiled=True)  68.4 us
    all_gather x1, waiting for transfers between devices, shards(): grad_block = lax.all_gather(pre_grad, 'row', axis=0, tiled=True)  59.6 us
    dot_general x8, matrix products, visit_group(): return running + jnp.einsum('ob,bjw->ojw', select, products)  51 us
    gather x8, local copies, waits for them, and re-layouts, visit_group(): gathered = blocked[source]  31.1 us
    dot_general x8, matrix products, visit_group(): jnp.einsum(pattern, picked, gathered, preferred_element_type=jnp.float32)  30.3 us
  transfers between devices with their start and end apart: 5, of which 5 were waited for; matrix products, arithmetic and copies ran while one was open for 0% of the time, Pallas kernels for 0%

commit v1 on v0

v1 whole, which is shorter than its diff:
```python
import functools

import jax
import jax.numpy as jnp
from jax import lax
from jax.experimental import pallas as pl
from jax.experimental.pallas import tpu as pltpu
from jax.sharding import PartitionSpec as P

MESH = pl.DeviceIdType.MESH
BF16 = jnp.bfloat16
F32 = jnp.float32
NX, NY, NZL, NZH = 4, 4, 4, 2
NT = (((1,), (1,)), ((), ()))


def whole_kernel(
    inv,
    tiles_hbm,
    feats,
    pre,
    cot,
    weight,
    out,
    tiles,
    gathered,
    acc,
    part,
    from_x,
    to_z,
    from_z,
    pre_t,
    grad_t,
    own,
    sent,
    core_in,
    half,
    plane_in,
    z_in,
    final,
    tile_sem,
    ag_send,
    ag_recv,
    rx_send,
    rx_recv,
    rz_send,
    rz_recv,
    core_send,
    core_recv,
    plane_send,
    plane_recv,
    z_send,
    z_recv,
    fin_send,
    fin_recv,
    last_send,
    last_recv,
):
    r = lax.axis_index("row")
    c = lax.axis_index("col")
    x, zh = r // NZH, r % NZH
    zl, y, k = c // (2 * NY), (c // 2) % NY, c % 2
    z = zh * NZL + zl
    live_slots = tiles_hbm.shape[0]

    def device(x_, zh_, zl_, y_, k_):
        return (x_ * NZH + zh_, (zl_ * NY + y_) * 2 + k_)

    def slot(zl_, y_, k_):
        return (zl_ * NY + y_) * 2 + k_

    sibling = device(x, zh, zl, y, 1 - k)
    y_up = device(x, zh, zl, (y + 1) % NY, k)
    y_down = device(x, zh, zl, (y + NY - 1) % NY, k)
    plane = []
    for dx in range(NX):
        for dy in range(NY):
            if dx or dy:
                xx, yy = (x + dx) % NX, (y + dy) % NY
                plane.append((xx * NY + yy, device(xx, zh, zl, yy, k)))
    z_line = []
    for dz in range(1, NZH * NZL):
        zz = (z + dz) % (NZH * NZL)
        z_line.append((zz, device(x, zz // NZL, zz % NZL, y, k)))

    def send(src, dst, ssem, rsem, dev):
        copy = pltpu.make_async_remote_copy(
            src_ref=src, dst_ref=dst, send_sem=ssem, recv_sem=rsem, device_id=dev, device_id_type=MESH
        )
        copy.start()
        return copy

    def arrived(ref, ssem, rsem):
        pltpu.make_async_remote_copy(
            src_ref=ref, dst_ref=ref, send_sem=ssem, recv_sem=rsem, device_id=sibling, device_id_type=MESH
        ).wait_recv()

    load_tiles = pltpu.make_async_copy(tiles_hbm, tiles.at[pl.ds(0, live_slots)], tile_sem)
    load_tiles.start()

    barrier = pltpu.get_barrier_semaphore()
    greet = [sibling] + [d for _, d in plane] + [d for _, d in z_line]
    for dev in greet:
        pl.semaphore_signal(barrier, inc=1, device_id=dev, device_id_type=MESH)
    gathered[0, c] = cot[...].T
    gathered[1, c] = feats[...].T
    pre_t[...] = pre[...].T
    tiles[live_slots] = jnp.zeros(tiles.shape[1:], BF16)
    pl.semaphore_wait(barrier, len(greet))

    sends = []
    counts = [0, 0]

    def forward(w, s, dev):
        n = counts[w]
        counts[w] += 1
        ref = gathered.at[w, s]
        sends.append(send(ref, ref, ag_send.at[w, n], ag_recv.at[w, s], dev))

    def landed(w, s):
        arrived(gathered.at[w, s], ag_send.at[w, 0], ag_recv.at[w, s])

    def plane_of(d):
        return (zl + d) % NZL

    def own_rows(i):
        w, d = divmod(i, NZL)
        s = slot(plane_of(d), y, k)
        if d:
            landed(w, s)
        forward(w, s, y_up)
        forward(w, s, y_down)
        forward(w, s, sibling)

    def near_rows(i):
        w, d = divmod(i, NZL)
        below = slot(plane_of(d), (y + NY - 1) % NY, k)
        above = slot(plane_of(d), (y + 1) % NY, k)
        landed(w, below)
        if d < NZL // 2:
            forward(w, below, y_up)
        forward(w, below, sibling)
        landed(w, above)
        if d >= NZL // 2:
            forward(w, above, y_down)
        forward(w, above, sibling)

    def far_rows(i):
        w, d = divmod(i, NZL)
        far = slot(plane_of(d), (y + 2) % NY, k)
        landed(w, far)
        forward(w, far, sibling)

    def product(w, base, q):
        left = jnp.concatenate([gathered[w, base + j] for j in range(2 * NY)], axis=1)
        right = jnp.concatenate(
            [
                jnp.concatenate([tiles[inv[(base + j) * 8 + 2 * q + h]] for h in range(2)], axis=1)
                for j in range(2 * NY)
            ],
            axis=0,
        )
        return jnp.dot(left, right, preferred_element_type=F32)

    def multiply(i):
        w, d = divmod(i, NZL)
        for yy in range(NY):
            landed(w, slot(plane_of(d), yy, 1 - k))
        base = slot(plane_of(d), 0, 0)
        if d < NZL - 1:

            def one(q, carry):
                value = product(w, base, q)
                acc[w, q] = value if d == 0 else acc[w, q] + value
                return carry

            lax.fori_loop(0, NX, one, 0)
            return
        for j in range(NX):
            q = (x + 1 + j) % NX
            value = acc[w, q] + product(w, base, q)
            if j < NX - 1:
                part[w, j] = value.astype(BF16)
                dev = device(q, zh, zl, y, k)
                sends.append(send(part.at[w, j], from_x.at[w, j], rx_send.at[w, j], rx_recv.at[w, j], dev))
            else:
                acc[w, q] = value

    def x_sum(w, which):
        lanes = pl.ds(pl.multiple_of(which * 128, 128), 128)
        total = acc[w, x, :, lanes]
        for j in range(NX - 1):
            total = total + from_x[w, j, :, lanes].astype(F32)
        return total

    def over_x(w):
        for j in range(NX - 1):
            arrived(from_x.at[w, j], rx_send.at[w, j], rx_recv.at[w, j])
        to_z[w] = x_sum(w, 1 - zh).astype(BF16)
        sends.append(send(to_z.at[w], from_z.at[w], rz_send.at[w], rz_recv.at[w], device(x, 1 - zh, zl, y, k)))

    def over_z(w):
        kept = x_sum(w, zh)
        arrived(from_z.at[w], rz_send.at[w], rz_recv.at[w])
        return (kept + from_z[w].astype(F32)).astype(BF16)

    def local(w):
        agg = over_z(w)
        if w == 0:
            left = jnp.maximum(pre_t[...], jnp.zeros((), BF16))
            grad = lax.dot_general(left, agg, NT, preferred_element_type=F32)
        else:
            grad = lax.dot_general(agg, grad_t[...], NT, preferred_element_type=F32)
        own[w] = grad
        sent[w] = grad.astype(BF16)
        rows = pl.ds(pl.multiple_of((1 - k) * 256, 256), 256)
        sends.append(send(sent.at[w, rows], core_in.at[w], core_send.at[w], core_recv.at[w], sibling))
        if w == 0:
            hidden = jnp.dot(weight[...], agg, preferred_element_type=F32)
            grad_t[...] = jnp.where(pre_t[...] > 0, hidden, 0.0).astype(BF16)

    me = x * NY + y

    def core_sum(w):
        arrived(core_in.at[w], core_send.at[w], core_recv.at[w])
        rows = pl.ds(pl.multiple_of(k * 256, 256), 256)
        total = own[w, rows] + core_in[w].astype(F32)
        half[w] = total.astype(BF16).reshape(NX * NY, 16, 512)
        for m, dev in plane:
            sends.append(
                send(half.at[w, m], plane_in.at[w, me], plane_send.at[w, m], plane_recv.at[w, me], dev)
            )

    def plane_sum(w):
        total = half[w, me].astype(F32)
        for m, _ in plane:
            arrived(plane_in.at[w, m], plane_send.at[w, m], plane_recv.at[w, m])
            total = total + plane_in[w, m].astype(F32)
        z_in[w, z] = total.astype(BF16)
        for zz, dev in z_line:
            sends.append(send(z_in.at[w, z], z_in.at[w, z], z_send.at[w, zz], z_recv.at[w, z], dev))

    def z_sum(w):
        for zz, _ in z_line:
            arrived(z_in.at[w, zz], z_send.at[w, zz], z_recv.at[w, zz])
        total = z_in[w, 0].astype(F32)
        for zz in range(1, NZH * NZL):
            total = total + z_in[w, zz].astype(F32)
        final[w, k, me] = total.astype(BF16)
        for m, dev in plane:
            ref = final.at[w, k, me]
            sends.append(send(ref, ref, fin_send.at[w, m], fin_recv.at[w, me], dev))

    def share(w):
        for m, _ in plane:
            arrived(final.at[w, k, m], fin_send.at[w, m], fin_recv.at[w, m])
        ref = final.at[w, k]
        sends.append(send(ref, ref, last_send.at[w], last_recv.at[w], sibling))

    def finish(w):
        arrived(final.at[w, 1 - k], last_send.at[w], last_recv.at[w])
        out[w] = final[w].reshape(512, 512)

    for w in range(2):
        for d in range(1, NZL):
            forward(w, c, device(x, zh, (zl + d) % NZL, y, k))
    load_tiles.wait()

    steps = 2 * NZL
    for i in range(steps + 3):
        if i < steps:
            own_rows(i)
        if 0 <= i - 1 < steps:
            near_rows(i - 1)
        if 0 <= i - 2 < steps:
            far_rows(i - 2)
        if 0 <= i - 3 < steps:
            multiply(i - 3)
        if i == NZL + 4:
            over_x(0)
        if i == NZL + 5:
            local(0)
    core_sum(0)
    over_x(1)
    plane_sum(0)
    local(1)
    core_sum(1)
    z_sum(0)
    plane_sum(1)
    share(0)
    z_sum(1)
    finish(0)
    share(1)
    finish(1)
    for copy in sends:
        copy.wait_send()


def shards(adj_tiles, tile_row, tile_col, tile_count, node_feats, pre_act, out_grad, second_weight):
    tiles = adj_tiles[0, 0]
    slots = tiles.shape[0]
    live = jnp.arange(slots, dtype=jnp.int32) < tile_count[0, 0]
    place = jnp.where(live, tile_row[0, 0] * 8 + tile_col[0, 0], -1)
    hit = place[None, :] == jnp.arange(256, dtype=jnp.int32)[:, None]
    inv = jnp.min(jnp.where(hit, jnp.arange(slots, dtype=jnp.int32)[None, :], slots), axis=1)
    vmem = pl.BlockSpec(memory_space=pltpu.VMEM)
    dma = pltpu.SemaphoreType.DMA
    result = pl.pallas_call(
        whole_kernel,
        out_shape=jax.ShapeDtypeStruct((2, 512, 512), BF16),
        in_specs=[pl.BlockSpec(memory_space=pltpu.SMEM), pl.BlockSpec(memory_space=pl.ANY)] + [vmem] * 4,
        out_specs=vmem,
        scratch_shapes=[
            pltpu.VMEM((slots + 1, 128, 128), BF16),
            pltpu.VMEM((2, 32, 512, 128), BF16),
            pltpu.VMEM((2, 4, 512, 256), F32),
            pltpu.VMEM((2, 3, 512, 256), BF16),
            pltpu.VMEM((2, 3, 512, 256), BF16),
            pltpu.VMEM((2, 512, 128), BF16),
            pltpu.VMEM((2, 512, 128), BF16),
            pltpu.VMEM((512, 128), BF16),
            pltpu.VMEM((512, 128), BF16),
            pltpu.VMEM((2, 512, 512), F32),
            pltpu.VMEM((2, 512, 512), BF16),
            pltpu.VMEM((2, 256, 512), BF16),
            pltpu.VMEM((2, 16, 16, 512), BF16),
            pltpu.VMEM((2, 16, 16, 512), BF16),
            pltpu.VMEM((2, 8, 16, 512), BF16),
            pltpu.VMEM((2, 2, 16, 16, 512), BF16),
            dma,
            dma((2, 31)),
            dma((2, 32)),
            dma((2, 3)),
            dma((2, 3)),
            dma((2,)),
            dma((2,)),
            dma((2,)),
            dma((2,)),
            dma((2, 16)),
            dma((2, 16)),
            dma((2, 8)),
            dma((2, 8)),
            dma((2, 16)),
            dma((2, 16)),
            dma((2,)),
            dma((2,)),
        ],
        compiler_params=pltpu.CompilerParams(
            collective_id=0, has_side_effects=True, vmem_limit_bytes=56 * 1024 * 1024
        ),
    )(inv, tiles, node_feats, pre_act, out_grad, second_weight)
    return result[1].astype(F32), result[0].astype(F32)


def solution(mesh):
    in_specs = (
        P("row", "col", None, None, None),
        P("row", "col", None),
        P("row", "col", None),
        P("row", "col"),
        P(("row", "col"), None),
        P(("col", "row"), None),
        P(("row", "col"), None),
        P(),
    )
    out_specs = (P(), P())
    return jax.shard_map(shards, mesh=mesh, in_specs=in_specs, out_specs=out_specs, check_vma=False)
```

time: 813 us -> 129 us (0.16)
  waiting for transfers between devices: 647 us -> 0 us
  Pallas kernels: 0 us -> 124 us
  matrix products: 86.6 us -> 0 us
  local copies, waits for them, and re-layouts: 53.8 us -> 0 us
  between operations: 14.5 us -> 1.29 us
    psum x1 -> x0, waiting for transfers between devices: 266 us -> none  [shards(): grad_first = lax.psum(first_part, ('row', 'col'))]
    reduce_scatter x2 -> x0, waiting for transfers between devices: 252 us -> none  [the longest x1 156 us: shards(): lax.psum_scatter(fwd_part.astype(jnp.bfloat16), 'col', scatter_dimension=...]
    all_gather x2 -> x0, waiting for transfers between devices: 128 us -> none  [the longest x1 68.4 us: shards(): cot_block = lax.all_gather(out_grad, 'col', axis=0, tiled=True)]
    pallas_call x0 -> x1, Pallas kernels: none -> 124 us  [shards(): pl.pallas_call(whole_kernel, out_shape=jax.ShapeDtypeStruct((2, 512, 512)...]
    dot_general x19 -> x0, matrix products: 86.6 us -> none  [the longest x8 51 us: visit_group(): return running + jnp.einsum('ob,bjw->ojw', select, products)]
    gather x8 -> x0, local copies, waits for them, and re-layouts: 31.1 us -> none  [visit_group(): gathered = blocked[source]]
    while x10 -> x0, local copies, waits for them, and re-layouts: 11.9 us -> none  [the longest x2 11.9 us: block_product(): running = lax.fori_loop(0, turn_count, visit_group, initial)]
  transfers between devices with their start and end apart: 5 -> 0, of which waited for: 5 -> 0; matrix products, arithmetic and copies ran while one was open for 0% -> 0% of each run, Pallas kernels for 0% -> 0%
where the time goes in v1:
time: 129 us
  Pallas kernels  124 us (96%)
  other arithmetic  4.18 us (3%)
  between operations  1.29 us (1%)
    pallas_call x1, Pallas kernels, shards(): pl.pallas_call(whole_kernel, out_shape=jax.ShapeDtypeStruct((2, 512, 512)...  124 us
    convert_element_type x1, other arithmetic, shards(): return (result[1].astype(F32), result[0].astype(F32))  2.81 us

profile of v1, /device:TPU:1, one launch (start us, length us, event | category | flops | bytes accessed | tf_op | source)
XLA Modules:
  0.0 129.3 jit_solution(16087490395375676402)
XLA Ops:
  1.3 0.7 multiply_add_fusion
  2.0 0.7 select_reduce_fusion.inv
  2.7 123.8 %shard_map.95 = bf16[2,512,512]{2,1,0:T(8,128)(2,1)} custom-call(s32[256]{0:T(256)} %select_reduce_fusion.inv, bf16[160,128,128]{2,1,0:T(8,128)(2,1)} %bitcast.10, bf16[128,512]{1,0:T(8,128)(2,1)} %feats.1, bf16[128,512]{1,0:T(8,128)(2,1)} %pre.1, bf16[128,512]{1,0:T(8,128)(2,1)} %cot.1, bf16[512,512]{1,0:T(8,128)(2,1)} %weight.1), custom_call_target="tpu_custom_call" | custom-call | tf_op jit(solution)/shard_map/pallas_call | solution.py:308
  126.5 2.8 %bitcast_convert_fusion = (f32[512,512]{1,0:T(8,128)}, f32[512,512]{1,0:T(8,128)}) fusion(bf16[2,512,512]{2,1,0:T(8,128)(2,1)} %shard_map.95), kind=kLoop, calls=%fused_computation | loop fusion | flops 524288 | bytes 3145728 | tf_op jit(solution)/shard_map/convert_element_type | solution.py:352
  (1 shorter events, 0.0 us)

commit v2 on v0

v2 whole, which is shorter than its diff:
```python
import functools

import jax
import jax.numpy as jnp
from jax import lax
from jax.experimental import pallas as pl
from jax.experimental.pallas import tpu as pltpu
from jax.sharding import PartitionSpec as P

MESH = pl.DeviceIdType.MESH
BF16 = jnp.bfloat16
F32 = jnp.float32
NX, NY, NZL, NZH = 4, 4, 4, 2
CHUNKS = 4
HALF = 256
UNIT_ROWS = (512, 256, 256)
UNIT_START = (0, 512, 768)
NT = (((1,), (1,)), ((), ()))


def whole_kernel(inv, tiles_hbm, feats, pre, cot, weight, out, *scratch):
    (tiles, gathered, acc, part, from_x, to_z, from_z, agg, pre_t, grad_t, z_in0, z_in1, z_in2) = scratch[:13]
    z_in = (z_in0, z_in1, z_in2)
    kept, given, core_in, piece, plane_in, final = (scratch[13 + 3 * n : 16 + 3 * n] for n in range(6))
    (tile_sem, ag_send, ag_recv, rx_send, rx_recv, rz_send, rz_recv) = scratch[31:38]
    (core_send, core_recv, plane_send, plane_recv, z_send, z_recv) = scratch[38:44]
    (fin_send, fin_recv, last_send, last_recv) = scratch[44:]
    r = lax.axis_index("row")
    c = lax.axis_index("col")
    x, zh = r // NZH, r % NZH
    zl, y, k = c // (2 * NY), (c // 2) % NY, c % 2
    z = zh * NZL + zl
    live_slots = tiles_hbm.shape[0]

    def device(x_, zh_, zl_, y_, k_):
        return (x_ * NZH + zh_, (zl_ * NY + y_) * 2 + k_)

    def slot(zl_, y_, k_):
        return (zl_ * NY + y_) * 2 + k_

    sibling = device(x, zh, zl, y, 1 - k)
    y_up = device(x, zh, zl, (y + 1) % NY, k)
    y_down = device(x, zh, zl, (y + NY - 1) % NY, k)
    plane = []
    for dx in range(NX):
        for dy in range(NY):
            if dx or dy:
                xx, yy = (x + dx) % NX, (y + dy) % NY
                plane.append((xx * NY + yy, device(xx, zh, zl, yy, k)))
    z_line = []
    for dz in range(1, NZH * NZL):
        zz = (z + dz) % (NZH * NZL)
        z_line.append((zz, device(x, zz // NZL, zz % NZL, y, k)))
    me = x * NY + y

    sends = []

    def send(src, dst, ssem, rsem, dev):
        copy = pltpu.make_async_remote_copy(
            src_ref=src, dst_ref=dst, send_sem=ssem, recv_sem=rsem, device_id=dev, device_id_type=MESH
        )
        copy.start()
        sends.append(copy)

    def arrived(ref, ssem, rsem):
        pltpu.make_async_remote_copy(
            src_ref=ref, dst_ref=ref, send_sem=ssem, recv_sem=rsem, device_id=sibling, device_id_type=MESH
        ).wait_recv()

    load_tiles = pltpu.make_async_copy(tiles_hbm, tiles.at[pl.ds(0, live_slots)], tile_sem)
    load_tiles.start()

    barrier = pltpu.get_barrier_semaphore()
    greet = [sibling] + [d for _, d in plane] + [d for _, d in z_line]
    for dev in greet:
        pl.semaphore_signal(barrier, inc=1, device_id=dev, device_id_type=MESH)
    for w, source in enumerate((cot, feats)):
        turned = source[...].T
        gathered[2 * w, c] = turned[:HALF]
        gathered[2 * w + 1, c] = turned[HALF:]
    pre_t[...] = pre[...].T
    tiles[live_slots] = jnp.zeros(tiles.shape[1:], BF16)
    pl.semaphore_wait(barrier, len(greet))

    counts = [0] * CHUNKS

    def forward(ch, s, dev):
        n = counts[ch]
        counts[ch] += 1
        ref = gathered.at[ch, s]
        send(ref, ref, ag_send.at[ch, n], ag_recv.at[ch, s], dev)

    def landed(ch, s):
        arrived(gathered.at[ch, s], ag_send.at[ch, 0], ag_recv.at[ch, s])

    def plane_of(d):
        return (zl + d) % NZL

    def spread(ch, s):
        forward(ch, s, y_up)
        forward(ch, s, y_down)
        forward(ch, s, sibling)

    def own_rows(ch, d):
        if d:
            s = slot(plane_of(d), y, k)
            landed(ch, s)
            spread(ch, s)

    def near_rows(ch, d):
        turn = (k + d) % 2
        first = slot(plane_of(d), (y + NY - 1 + 2 * turn) % NY, k)
        second = slot(plane_of(d), (y + 1 + 2 * turn) % NY, k)
        landed(ch, first)
        forward(ch, first, device(x, zh, zl, (y + 1 + 2 * turn) % NY, k))
        forward(ch, first, sibling)
        landed(ch, second)
        forward(ch, second, sibling)

    def far_rows(ch, d):
        far = slot(plane_of(d), (y + 2) % NY, k)
        landed(ch, far)
        forward(ch, far, sibling)

    def product(ch, base, q):
        left = jnp.concatenate([gathered[ch, base + j] for j in range(2 * NY)], axis=1)
        right = jnp.concatenate(
            [
                jnp.concatenate([tiles[inv[(base + j) * 8 + 2 * q + h]] for h in range(2)], axis=1)
                for j in range(2 * NY)
            ],
            axis=0,
        )
        return jnp.dot(left, right, preferred_element_type=F32)

    def multiply(ch, d):
        for yy in range(NY):
            landed(ch, slot(plane_of(d), yy, 1 - k))
        base = slot(plane_of(d), 0, 0)
        if d < NZL - 1:

            def one(q, carry):
                value = product(ch, base, q)
                acc[ch, q] = value if d == 0 else acc[ch, q] + value
                return carry

            lax.fori_loop(0, NX, one, 0)
            return
        for j in range(NX):
            q = (x + 1 + j) % NX
            value = acc[ch, q] + product(ch, base, q)
            if j < NX - 1:
                part[ch, j] = value.astype(BF16)
                dev = device(q, zh, zl, y, k)
                send(part.at[ch, j], from_x.at[ch, j], rx_send.at[ch, j], rx_recv.at[ch, j], dev)
            else:
                acc[ch, q] = value

    def x_sum(ch, which):
        lanes = pl.ds(pl.multiple_of(which * 128, 128), 128)
        total = acc[ch, x, :, lanes]
        for j in range(NX - 1):
            total = total + from_x[ch, j, :, lanes].astype(F32)
        return total

    def over_x(ch):
        for j in range(NX - 1):
            arrived(from_x.at[ch, j], rx_send.at[ch, j], rx_recv.at[ch, j])
        to_z[ch] = x_sum(ch, 1 - zh).astype(BF16)
        send(to_z.at[ch], from_z.at[ch], rz_send.at[ch], rz_recv.at[ch], device(x, 1 - zh, zl, y, k))

    def over_z(ch):
        total = x_sum(ch, zh)
        arrived(from_z.at[ch], rz_send.at[ch], rz_recv.at[ch])
        rows = pl.ds((ch % 2) * HALF, HALF)
        agg[ch // 2, rows] = (total + from_z[ch].astype(F32)).astype(BF16)

    def local(u):
        rows = UNIT_ROWS[u] // 2

        def share_of(core):
            start = pl.multiple_of(core * rows, rows)
            if u == 0:
                left = jnp.maximum(pre_t[pl.ds(start, rows)], jnp.zeros((), BF16))
                right = agg[0]
            else:
                left = agg[1, pl.ds((u - 1) * HALF + start, rows)]
                right = grad_t[...]
            return lax.dot_general(left, right, NT, preferred_element_type=F32)

        given[u][...] = share_of(1 - k).astype(BF16)
        send(given[u], core_in[u], core_send.at[u], core_recv.at[u], sibling)
        kept[u][...] = share_of(k)
        if u == 0:
            hidden = jnp.dot(weight[...], agg[0], preferred_element_type=F32)
            grad_t[...] = jnp.where(pre_t[...] > 0, hidden, 0.0).astype(BF16)

    def core_sum(u):
        arrived(core_in[u], core_send.at[u], core_recv.at[u])
        total = (kept[u][...] + core_in[u][...].astype(F32)).astype(BF16)
        wide = UNIT_ROWS[u]
        cuts = 512 // wide
        for m in range(NX * NY):
            top, left = (m // cuts) * 16, (m % cuts) * wide
            piece[u][m] = total[top : top + 16, left : left + wide]
        for m, dev in plane:
            send(piece[u].at[m], plane_in[u].at[me], plane_send.at[u, m], plane_recv.at[u, me], dev)

    def plane_sum(u):
        total = piece[u][me].astype(F32)
        for m, _ in plane:
            arrived(plane_in[u].at[m], plane_send.at[u, m], plane_recv.at[u, m])
            total = total + plane_in[u][m].astype(F32)
        z_in[u][z] = total.astype(BF16)
        for zz, dev in z_line:
            send(z_in[u].at[z], z_in[u].at[z], z_send.at[u, zz], z_recv.at[u, z], dev)

    def z_sum(u):
        for zz, _ in z_line:
            arrived(z_in[u].at[zz], z_send.at[u, zz], z_recv.at[u, zz])
        total = z_in[u][0].astype(F32)
        for zz in range(1, NZH * NZL):
            total = total + z_in[u][zz].astype(F32)
        final[u][k, me] = total.astype(BF16)
        ref = final[u].at[k, me]
        for m, dev in plane:
            send(ref, ref, fin_send.at[u, m], fin_recv.at[u, me], dev)

    def share(u):
        for m, _ in plane:
            arrived(final[u].at[k, m], fin_send.at[u, m], fin_recv.at[u, m])
        ref = final[u].at[k]
        send(ref, ref, last_send.at[u], last_recv.at[u], sibling)

    def finish(u):
        arrived(final[u].at[1 - k], last_send.at[u], last_recv.at[u])
        wide = UNIT_ROWS[u]
        cuts = 512 // wide
        base = UNIT_START[u]
        for core in range(2):
            for m in range(NX * NY):
                top, left = base + core * (wide // 2) + (m // cuts) * 16, (m % cuts) * wide
                out[top : top + 16, left : left + wide] = final[u][core, m]

    for ch in range(CHUNKS):
        for d in range(NZL - 1, 0, -1):
            forward(ch, c, device(x, zh, (zl + d) % NZL, y, k))
    for ch in range(CHUNKS):
        spread(ch, c)
    load_tiles.wait()

    steps = [(ch, d) for ch in range(CHUNKS) for d in range(NZL)]
    for i in range(len(steps) + 7):
        for lag, job in ((0, own_rows), (3, near_rows), (6, far_rows)):
            if 0 <= i - lag < len(steps):
                job(*steps[i - lag])
        if i >= 14 and (i - 14) % NZL == 0 and (i - 14) // NZL < CHUNKS:
            over_x((i - 14) // NZL)
        if i == 17:
            over_z(0)
        if i == 21:
            over_z(1)
            local(0)
        if i >= 7:
            multiply(*steps[i - 7])
    core_sum(0)
    over_z(2)
    local(1)
    core_sum(1)
    over_x(3)
    plane_sum(0)
    plane_sum(1)
    over_z(3)
    local(2)
    z_sum(0)
    core_sum(2)
    z_sum(1)
    share(0)
    plane_sum(2)
    share(1)
    finish(0)
    z_sum(2)
    finish(1)
    share(2)
    finish(2)
    for copy in sends:
        copy.wait_send()


def shards(adj_tiles, tile_row, tile_col, tile_count, node_feats, pre_act, out_grad, second_weight):
    tiles = adj_tiles[0, 0]
    slots = tiles.shape[0]
    live = jnp.arange(slots, dtype=jnp.int32) < tile_count[0, 0]
    place = jnp.where(live, tile_row[0, 0] * 8 + tile_col[0, 0], -1)
    hit = place[None, :] == jnp.arange(256, dtype=jnp.int32)[:, None]
    inv = jnp.min(jnp.where(hit, jnp.arange(slots, dtype=jnp.int32)[None, :], slots), axis=1)
    vmem = pl.BlockSpec(memory_space=pltpu.VMEM)
    dma = pltpu.SemaphoreType.DMA
    result = pl.pallas_call(
        whole_kernel,
        out_shape=jax.ShapeDtypeStruct((1024, 512), BF16),
        in_specs=[pl.BlockSpec(memory_space=pltpu.SMEM), pl.BlockSpec(memory_space=pl.ANY)] + [vmem] * 4,
        out_specs=vmem,
        scratch_shapes=[
            pltpu.VMEM((slots + 1, 128, 128), BF16),
            pltpu.VMEM((CHUNKS, 32, HALF, 128), BF16),
            pltpu.VMEM((CHUNKS, NX, HALF, 256), F32),
            pltpu.VMEM((CHUNKS, 3, HALF, 256), BF16),
            pltpu.VMEM((CHUNKS, 3, HALF, 256), BF16),
            pltpu.VMEM((CHUNKS, HALF, 128), BF16),
            pltpu.VMEM((CHUNKS, HALF, 128), BF16),
            pltpu.VMEM((2, 512, 128), BF16),
            pltpu.VMEM((512, 128), BF16),
            pltpu.VMEM((512, 128), BF16),
        ]
        + [pltpu.VMEM((8, 16, n), BF16) for n in UNIT_ROWS]
        + [pltpu.VMEM((n // 2, 512), F32) for n in UNIT_ROWS]
        + [pltpu.VMEM((n // 2, 512), BF16) for n in UNIT_ROWS]
        + [pltpu.VMEM((n // 2, 512), BF16) for n in UNIT_ROWS]
        + [pltpu.VMEM((16, 16, n), BF16) for n in UNIT_ROWS]
        + [pltpu.VMEM((16, 16, n), BF16) for n in UNIT_ROWS]
        + [pltpu.VMEM((2, 16, 16, n), BF16) for n in UNIT_ROWS]
        + [
            dma,
            dma((CHUNKS, 31)),
            dma((CHUNKS, 32)),
            dma((CHUNKS, 3)),
            dma((CHUNKS, 3)),
            dma((CHUNKS,)),
            dma((CHUNKS,)),
            dma((3,)),
            dma((3,)),
            dma((3, 16)),
            dma((3, 16)),
            dma((3, 8)),
            dma((3, 8)),
            dma((3, 16)),
            dma((3, 16)),
            dma((3,)),
            dma((3,)),
        ],
        compiler_params=pltpu.CompilerParams(
            collective_id=0, has_side_effects=True, vmem_limit_bytes=56 * 1024 * 1024
        ),
    )(inv, tiles, node_feats, pre_act, out_grad, second_weight)
    return result[512:].astype(F32), result[:512].astype(F32)


def solution(mesh):
    in_specs = (
        P("row", "col", None, None, None),
        P("row", "col", None),
        P("row", "col", None),
        P("row", "col"),
        P(("row", "col"), None),
        P(("col", "row"), None),
        P(("row", "col"), None),
        P(),
    )
    out_specs = (P(), P())
    return jax.shard_map(shards, mesh=mesh, in_specs=in_specs, out_specs=out_specs, check_vma=False)
```

time: 813 us -> 113 us (0.14)
  waiting for transfers between devices: 647 us -> 0 us
  Pallas kernels: 0 us -> 107 us
  matrix products: 86.6 us -> 0 us
  local copies, waits for them, and re-layouts: 53.8 us -> 0 us
  between operations: 14.5 us -> 1.29 us
    psum x1 -> x0, waiting for transfers between devices: 266 us -> none  [shards(): grad_first = lax.psum(first_part, ('row', 'col'))]
    reduce_scatter x2 -> x0, waiting for transfers between devices: 252 us -> none  [the longest x1 156 us: shards(): lax.psum_scatter(fwd_part.astype(jnp.bfloat16), 'col', scatter_dimension=...]
    all_gather x2 -> x0, waiting for transfers between devices: 128 us -> none  [the longest x1 68.4 us: shards(): cot_block = lax.all_gather(out_grad, 'col', axis=0, tiled=True)]
    pallas_call x0 -> x1, Pallas kernels: none -> 107 us  [shards(): pl.pallas_call(whole_kernel, out_shape=jax.ShapeDtypeStruct((1024, 512),...]
    dot_general x19 -> x0, matrix products: 86.6 us -> none  [the longest x8 51 us: visit_group(): return running + jnp.einsum('ob,bjw->ojw', select, products)]
    gather x8 -> x0, local copies, waits for them, and re-layouts: 31.1 us -> none  [visit_group(): gathered = blocked[source]]
    while x10 -> x0, local copies, waits for them, and re-layouts: 11.9 us -> none  [the longest x2 11.9 us: block_product(): running = lax.fori_loop(0, turn_count, visit_group, initial)]
  transfers between devices with their start and end apart: 5 -> 0, of which waited for: 5 -> 0; matrix products, arithmetic and copies ran while one was open for 0% -> 0% of each run, Pallas kernels for 0% -> 0%
where the time goes in v2:
time: 113 us
  Pallas kernels  107 us (95%)
  other arithmetic  4.18 us (4%)
  between operations  1.29 us (1%)
    pallas_call x1, Pallas kernels, shards(): pl.pallas_call(whole_kernel, out_shape=jax.ShapeDtypeStruct((1024, 512),...  107 us
    convert_element_type x1, other arithmetic, shards(): return (result[512:].astype(F32), result[:512].astype(F32))  2.81 us

profile of v2, /device:TPU:1, one launch (start us, length us, event | category | flops | bytes accessed | tf_op | source)
XLA Modules:
  0.0 112.5 jit_solution(13853582724268761500)
XLA Ops:
  1.3 0.7 multiply_add_fusion
  2.0 0.7 select_reduce_fusion.inv
  2.7 107.0 %shard_map.95 = bf16[1024,512]{1,0:T(8,128)(2,1)} custom-call(s32[256]{0:T(256)} %select_reduce_fusion.inv, bf16[160,128,128]{2,1,0:T(8,128)(2,1)} %bitcast.4, bf16[128,512]{1,0:T(8,128)(2,1)} %feats.1, bf16[128,512]{1,0:T(8,128)(2,1)} %pre.1, bf16[128,512]{1,0:T(8,128)(2,1)} %cot.1, bf16[512,512]{1,0:T(8,128)(2,1)} %weight.1), custom_call_target="tpu_custom_call" | custom-call | tf_op jit(solution)/shard_map/pallas_call | solution.py:299
  109.7 2.8 %slice_convert_fusion = (f32[512,512]{1,0:T(8,128)}, f32[512,512]{1,0:T(8,128)}) fusion(bf16[1024,512]{1,0:T(8,128)(2,1)} %shard_map.95), kind=kLoop, calls=%fused_computation | loop fusion | flops 524288 | bytes 3145728 | tf_op jit(solution)/shard_map/convert_element_type | solution.py:346
  (1 shorter events, 0.0 us)

commit v3 on v2

--- a/solution.py
+++ b/solution.py
@@ -11,20 +11,31 @@
 BF16 = jnp.bfloat16
 F32 = jnp.float32
 NX, NY, NZL, NZH = 4, 4, 4, 2
-CHUNKS = 4
-HALF = 256
+WIDTH = (256, 256, 256, 128, 128)
+START = (0, 256, 0, 256, 384)
+SIDE = (0, 0, 1, 1, 1)
+CHUNKS = len(WIDTH)
 UNIT_ROWS = (512, 256, 256)
 UNIT_START = (0, 512, 768)
+UNITS = len(UNIT_ROWS)
 NT = (((1,), (1,)), ((), ()))
 
 
-def whole_kernel(inv, tiles_hbm, feats, pre, cot, weight, out, *scratch):
-    (tiles, gathered, acc, part, from_x, to_z, from_z, agg, pre_t, grad_t, z_in0, z_in1, z_in2) = scratch[:13]
-    z_in = (z_in0, z_in1, z_in2)
-    kept, given, core_in, piece, plane_in, final = (scratch[13 + 3 * n : 16 + 3 * n] for n in range(6))
-    (tile_sem, ag_send, ag_recv, rx_send, rx_recv, rz_send, rz_recv) = scratch[31:38]
-    (core_send, core_recv, plane_send, plane_recv, z_send, z_recv) = scratch[38:44]
-    (fin_send, fin_recv, last_send, last_recv) = scratch[44:]
+def whole_kernel(row_hbm, col_hbm, live, tiles_hbm, feats_hbm, pre_hbm, cot_hbm, weight_hbm, out, *scratch):
+    scratch = list(scratch)
+
+    def take(n=None):
+        if n is None:
+            return scratch.pop(0)
+        return [scratch.pop(0) for _ in range(n)]
+
+    tiles, feats, pre, cot, weight, places, table, inv = take(8)
+    gathered, acc, part, from_x, to_z, from_z = (take(CHUNKS) for _ in range(6))
+    agg, pre_t, grad_t = take(3)
+    z_in, kept, given, core_in, piece, plane_in, final = (take(UNITS) for _ in range(7))
+    tile_sem, load_sem, ag_send, ag_recv, rx_send, rx_recv, rz_send, rz_recv = take(8)
+    core_send, core_recv, plane_send, plane_recv, z_send, z_recv = take(6)
+    fin_send, fin_recv, last_send, last_recv = take(4)
     r = lax.axis_index("row")
     c = lax.axis_index("col")
     x, zh = r // NZH, r % NZH
@@ -67,19 +78,48 @@
             src_ref=ref, dst_ref=ref, send_sem=ssem, recv_sem=rsem, device_id=sibling, device_id_type=MESH
         ).wait_recv()
 
-    load_tiles = pltpu.make_async_copy(tiles_hbm, tiles.at[pl.ds(0, live_slots)], tile_sem)
+    load_tiles = pltpu.make_async_copy(tiles_hbm, tiles.at[pl.ds(0, live_slots)], tile_sem.at[0])
+    loads = [
+        pltpu.make_async_copy(src, dst, load_sem.at[n])
+        for n, (src, dst) in enumerate(
+            [
+                (cot_hbm, cot),
+                (feats_hbm, feats),
+                (row_hbm, places.at[0]),
+                (col_hbm, places.at[1]),
+                (pre_hbm, pre),
+                (weight_hbm, weight),
+            ]
+        )
+    ]
+    for copy in loads:
+        copy.start()
     load_tiles.start()
 
     barrier = pltpu.get_barrier_semaphore()
-    greet = [sibling] + [d for _, d in plane] + [d for _, d in z_line]
+    greet = [d for _, d in z_line] + [d for _, d in plane] + [sibling]
     for dev in greet:
         pl.semaphore_signal(barrier, inc=1, device_id=dev, device_id_type=MESH)
-    for w, source in enumerate((cot, feats)):
+    for side, source in enumerate((cot, feats)):
+        loads[side].wait()
         turned = source[...].T
-        gathered[2 * w, c] = turned[:HALF]
-        gathered[2 * w + 1, c] = turned[HALF:]
+        for ch in range(CHUNKS):
+            if SIDE[ch] == side:
+                gathered[ch][c] = turned[START[ch] : START[ch] + WIDTH[ch]]
+    loads[2].wait()
+    loads[3].wait()
+    turn = lax.broadcasted_iota(jnp.int32, (1, live_slots), 1)
+    place = jnp.where(turn < live[0, 0], places[0] * 8 + places[1], -1)
+    hit = place == lax.broadcasted_iota(jnp.int32, (256, live_slots), 0)
+    found = jnp.min(jnp.where(hit, turn, live_slots), axis=1, keepdims=True)
+    table[...] = jnp.broadcast_to(found, (256, 128)).T[0:8]
+    to_scalar = pltpu.make_async_copy(table, inv, tile_sem.at[1])
+    to_scalar.start()
+    tiles[live_slots] = jnp.zeros(tiles.shape[1:], BF16)
+    loads[4].wait()
     pre_t[...] = pre[...].T
-    tiles[live_slots] = jnp.zeros(tiles.shape[1:], BF16)
+    loads[5].wait()
+    to_scalar.wait()
     pl.semaphore_wait(barrier, len(greet))
 
     counts = [0] * CHUNKS
@@ -87,11 +127,11 @@
     def forward(ch, s, dev):
         n = counts[ch]
         counts[ch] += 1
-        ref = gathered.at[ch, s]
+        ref = gathered[ch].at[s]
         send(ref, ref, ag_send.at[ch, n], ag_recv.at[ch, s], dev)
 
     def landed(ch, s):
-        arrived(gathered.at[ch, s], ag_send.at[ch, 0], ag_recv.at[ch, s])
+        arrived(gathered[ch].at[s], ag_send.at[ch, 0], ag_recv.at[ch, s])
 
     def plane_of(d):
         return (zl + d) % NZL
@@ -123,10 +163,10 @@
         forward(ch, far, sibling)
 
     def product(ch, base, q):
-        left = jnp.concatenate([gathered[ch, base + j] for j in range(2 * NY)], axis=1)
+        left = jnp.concatenate([gathered[ch][base + j] for j in range(2 * NY)], axis=1)
         right = jnp.concatenate(
             [
-                jnp.concatenate([tiles[inv[(base + j) * 8 + 2 * q + h]] for h in range(2)], axis=1)
+                jnp.concatenate([tiles[inv[0, (base + j) * 8 + 2 * q + h]] for h in range(2)], axis=1)
                 for j in range(2 * NY)
             ],
             axis=0,
@@ -141,39 +181,39 @@
 
             def one(q, carry):
                 value = product(ch, base, q)
-                acc[ch, q] = value if d == 0 else acc[ch, q] + value
+                acc[ch][q] = value if d == 0 else acc[ch][q] + value
                 return carry
 
             lax.fori_loop(0, NX, one, 0)
             return
         for j in range(NX):
             q = (x + 1 + j) % NX
-            value = acc[ch, q] + product(ch, base, q)
+            value = acc[ch][q] + product(ch, base, q)
             if j < NX - 1:
-                part[ch, j] = value.astype(BF16)
+                part[ch][j] = value.astype(BF16)
                 dev = device(q, zh, zl, y, k)
-                send(part.at[ch, j], from_x.at[ch, j], rx_send.at[ch, j], rx_recv.at[ch, j], dev)
+                send(part[ch].at[j], from_x[ch].at[j], rx_send.at[ch, j], rx_recv.at[ch, j], dev)
             else:
-                acc[ch, q] = value
+                acc[ch][q] = value
 
     def x_sum(ch, which):
         lanes = pl.ds(pl.multiple_of(which * 128, 128), 128)
-        total = acc[ch, x, :, lanes]
+        total = acc[ch][x, :, lanes]
         for j in range(NX - 1):
-            total = total + from_x[ch, j, :, lanes].astype(F32)
+            total = total + from_x[ch][j, :, lanes].astype(F32)
         return total
 
     def over_x(ch):
         for j in range(NX - 1):
-            arrived(from_x.at[ch, j], rx_send.at[ch, j], rx_recv.at[ch, j])
-        to_z[ch] = x_sum(ch, 1 - zh).astype(BF16)
-        send(to_z.at[ch], from_z.at[ch], rz_send.at[ch], rz_recv.at[ch], device(x, 1 - zh, zl, y, k))
+            arrived(from_x[ch].at[j], rx_send.at[ch, j], rx_recv.at[ch, j])
+        to_z[ch][...] = x_sum(ch, 1 - zh).astype(BF16)
+        send(to_z[ch], from_z[ch], rz_send.at[ch], rz_recv.at[ch], device(x, 1 - zh, zl, y, k))
 
     def over_z(ch):
         total = x_sum(ch, zh)
-        arrived(from_z.at[ch], rz_send.at[ch], rz_recv.at[ch])
-        rows = pl.ds((ch % 2) * HALF, HALF)
-        agg[ch // 2, rows] = (total + from_z[ch].astype(F32)).astype(BF16)
+        arrived(from_z[ch], rz_send.at[ch], rz_recv.at[ch])
+        rows = pl.ds(START[ch], WIDTH[ch])
+        agg[SIDE[ch], rows] = (total + from_z[ch][...].astype(F32)).astype(BF16)
 
     def local(u):
         rows = UNIT_ROWS[u] // 2
@@ -184,7 +224,7 @@
                 left = jnp.maximum(pre_t[pl.ds(start, rows)], jnp.zeros((), BF16))
                 right = agg[0]
             else:
-                left = agg[1, pl.ds((u - 1) * HALF + start, rows)]
+                left = agg[1, pl.ds(UNIT_START[u] - 512 + start, rows)]
                 right = grad_t[...]
             return lax.dot_general(left, right, NT, preferred_element_type=F32)
 
@@ -254,32 +294,35 @@
         for lag, job in ((0, own_rows), (3, near_rows), (6, far_rows)):
             if 0 <= i - lag < len(steps):
                 job(*steps[i - lag])
-        if i >= 14 and (i - 14) % NZL == 0 and (i - 14) // NZL < CHUNKS:
-            over_x((i - 14) // NZL)
         if i == 17:
+            over_x(0)
+        if i == 21:
+            over_x(1)
             over_z(0)
-        if i == 21:
-            over_z(1)
-            local(0)
         if i >= 7:
             multiply(*steps[i - 7])
+    over_x(2)
+    over_z(1)
+    local(0)
+    over_x(3)
     core_sum(0)
+    over_x(4)
     over_z(2)
     local(1)
+    plane_sum(0)
     core_sum(1)
-    over_x(3)
-    plane_sum(0)
-    plane_sum(1)
     over_z(3)
+    over_z(4)
     local(2)
     z_sum(0)
     core_sum(2)
-    z_sum(1)
+    plane_sum(1)
     share(0)
     plane_sum(2)
-    share(1)
+    z_sum(1)
     finish(0)
     z_sum(2)
+    share(1)
     finish(1)
     share(2)
     finish(2)
@@ -290,59 +333,63 @@
 def shards(adj_tiles, tile_row, tile_col, tile_count, node_feats, pre_act, out_grad, second_weight):
     tiles = adj_tiles[0, 0]
     slots = tiles.shape[0]
-    live = jnp.arange(slots, dtype=jnp.int32) < tile_count[0, 0]
-    place = jnp.where(live, tile_row[0, 0] * 8 + tile_col[0, 0], -1)
-    hit = place[None, :] == jnp.arange(256, dtype=jnp.int32)[:, None]
-    inv = jnp.min(jnp.where(hit, jnp.arange(slots, dtype=jnp.int32)[None, :], slots), axis=1)
-    vmem = pl.BlockSpec(memory_space=pltpu.VMEM)
+    vmem = pltpu.VMEM
     dma = pltpu.SemaphoreType.DMA
+    smem = pl.BlockSpec(memory_space=pltpu.SMEM)
+    hbm = pl.BlockSpec(memory_space=pl.ANY)
     result = pl.pallas_call(
         whole_kernel,
         out_shape=jax.ShapeDtypeStruct((1024, 512), BF16),
-        in_specs=[pl.BlockSpec(memory_space=pltpu.SMEM), pl.BlockSpec(memory_space=pl.ANY)] + [vmem] * 4,
-        out_specs=vmem,
+        in_specs=[hbm, hbm, smem] + [hbm] * 5,
+        out_specs=pl.BlockSpec(memory_space=pltpu.VMEM),
         scratch_shapes=[
-            pltpu.VMEM((slots + 1, 128, 128), BF16),
-            pltpu.VMEM((CHUNKS, 32, HALF, 128), BF16),
-            pltpu.VMEM((CHUNKS, NX, HALF, 256), F32),
-            pltpu.VMEM((CHUNKS, 3, HALF, 256), BF16),
-            pltpu.VMEM((CHUNKS, 3, HALF, 256), BF16),
-            pltpu.VMEM((CHUNKS, HALF, 128), BF16),
-            pltpu.VMEM((CHUNKS, HALF, 128), BF16),
-            pltpu.VMEM((2, 512, 128), BF16),
-            pltpu.VMEM((512, 128), BF16),
-            pltpu.VMEM((512, 128), BF16),
+            vmem((slots + 1, 128, 128), BF16),
+            vmem((128, 512), BF16),
+            vmem((128, 512), BF16),
+            vmem((128, 512), BF16),
+            vmem((512, 512), BF16),
+            vmem((2, 1, slots), jnp.int32),
+            vmem((8, 256), jnp.int32),
+            pltpu.SMEM((8, 256), jnp.int32),
         ]
-        + [pltpu.VMEM((8, 16, n), BF16) for n in UNIT_ROWS]
-        + [pltpu.VMEM((n // 2, 512), F32) for n in UNIT_ROWS]
-        + [pltpu.VMEM((n // 2, 512), BF16) for n in UNIT_ROWS]
-        + [pltpu.VMEM((n // 2, 512), BF16) for n in UNIT_ROWS]
-        + [pltpu.VMEM((16, 16, n), BF16) for n in UNIT_ROWS]
-        + [pltpu.VMEM((16, 16, n), BF16) for n in UNIT_ROWS]
-        + [pltpu.VMEM((2, 16, 16, n), BF16) for n in UNIT_ROWS]
+        + [vmem((32, n, 128), BF16) for n in WIDTH]
+        + [vmem((NX, n, 256), F32) for n in WIDTH]
+        + [vmem((3, n, 256), BF16) for n in WIDTH]
+        + [vmem((3, n, 256), BF16) for n in WIDTH]
+        + [vmem((n, 128), BF16) for n in WIDTH]
+        + [vmem((n, 128), BF16) for n in WIDTH]
+        + [vmem((2, 512, 128), BF16), vmem((512, 128), BF16), vmem((512, 128), BF16)]
+        + [vmem((8, 16, n), BF16) for n in UNIT_ROWS]
+        + [vmem((n // 2, 512), F32) for n in UNIT_ROWS]
+        + [vmem((n // 2, 512), BF16) for n in UNIT_ROWS]
+        + [vmem((n // 2, 512), BF16) for n in UNIT_ROWS]
+        + [vmem((16, 16, n), BF16) for n in UNIT_ROWS]
+        + [vmem((16, 16, n), BF16) for n in UNIT_ROWS]
+        + [vmem((2, 16, 16, n), BF16) for n in UNIT_ROWS]
         + [
-            dma,
+            dma((2,)),
+            dma((6,)),
             dma((CHUNKS, 31)),
             dma((CHUNKS, 32)),
             dma((CHUNKS, 3)),
             dma((CHUNKS, 3)),
             dma((CHUNKS,)),
             dma((CHUNKS,)),
-            dma((3,)),
-            dma((3,)),
-            dma((3, 16)),
-            dma((3, 16)),
-            dma((3, 8)),
-            dma((3, 8)),
-            dma((3, 16)),
-            dma((3, 16)),
-            dma((3,)),
-            dma((3,)),
+            dma((UNITS,)),
+            dma((UNITS,)),
+            dma((UNITS, 16)),
+            dma((UNITS, 16)),
+            dma((UNITS, 8)),
+            dma((UNITS, 8)),
+            dma((UNITS, 16)),
+            dma((UNITS, 16)),
+            dma((UNITS,)),
+            dma((UNITS,)),
         ],
         compiler_params=pltpu.CompilerParams(
             collective_id=0, has_side_effects=True, vmem_limit_bytes=56 * 1024 * 1024
         ),
-    )(inv, tiles, node_feats, pre_act, out_grad, second_weight)
+    )(tile_row[0], tile_col[0], tile_count, tiles, node_feats, pre_act, out_grad, second_weight)
     return result[512:].astype(F32), result[:512].astype(F32)
 
 

time: 113 us -> 105 us (0.929)
  Pallas kernels: 107 us -> 101 us
  other arithmetic: 4.18 us -> 2.81 us
    pallas_call x1, Pallas kernels: 107 us -> 101 us  [shards(): pl.pallas_call(whole_kernel, out_shape=jax.ShapeDtypeStruct((1024, 512),...]
where the time goes in v3:
time: 105 us
  Pallas kernels  101 us (96%)
  other arithmetic  2.81 us (3%)
  between operations  1.29 us (1%)
    pallas_call x1, Pallas kernels, shards(): pl.pallas_call(whole_kernel, out_shape=jax.ShapeDtypeStruct((1024, 512),...  101 us
    convert_element_type x1, other arithmetic, shards(): return (result[512:].astype(F32), result[:512].astype(F32))  2.81 us

profile of v3, /device:TPU:1, one launch (start us, length us, event | category | flops | bytes accessed | tf_op | source)
XLA Modules:
  0.0 105.2 jit_solution(16133107846816335896)
XLA Ops:
  1.3 101.1 %shard_map.95 = bf16[1024,512]{1,0:T(8,128)(2,1)} custom-call(s32[1,160]{1,0:T(1,128)} %bitcast.4, s32[1,160]{1,0:T(1,128)} %bitcast.5, s32[1,1]{1,0:T(1,128)S(6)} %copy.10.live, bf16[160,128,128]{2,1,0:T(8,128)(2,1)} %bitcast.3, bf16[128,512]{1,0:T(8,128)(2,1)} %feats_hbm.1, bf16[128,512]{1,0:T(8,128)(2,1)} %pre_hbm.1, bf16[128,512]{1,0:T(8,128)(2,1)} %cot_hbm.1, ...), custom_call_target="tpu_custom_call" | custom-call | tf_op jit(solution)/shard_map/pallas_call | solution.py:340
  102.4 2.8 %slice_convert_fusion = (f32[512,512]{1,0:T(8,128)}, f32[512,512]{1,0:T(8,128)}) fusion(bf16[1024,512]{1,0:T(8,128)(2,1)} %shard_map.95), kind=kLoop, calls=%fused_computation | loop fusion | flops 524288 | bytes 3145728 | tf_op jit(solution)/shard_map/convert_element_type | solution.py:393

commit v4 on v3

--- a/solution.py
+++ b/solution.py
@@ -53,13 +53,12 @@
     y_up = device(x, zh, zl, (y + 1) % NY, k)
     y_down = device(x, zh, zl, (y + NY - 1) % NY, k)
     plane = []
-    for dx in range(NX):
-        for dy in range(NY):
-            if dx or dy:
-                xx, yy = (x + dx) % NX, (y + dy) % NY
-                plane.append((xx * NY + yy, device(xx, zh, zl, yy, k)))
+    around = [(dx, dy) for dx in range(NX) for dy in range(NY) if dx or dy]
+    for dx, dy in sorted(around, key=lambda p: -min(p[0], NX - p[0]) - min(p[1], NY - p[1])):
+        xx, yy = (x + dx) % NX, (y + dy) % NY
+        plane.append((xx * NY + yy, device(xx, zh, zl, yy, k)))
     z_line = []
-    for dz in range(1, NZH * NZL):
+    for dz in sorted(range(1, NZH * NZL), key=lambda n: -min(n, NZH * NZL - n)):
         zz = (z + dz) % (NZH * NZL)
         z_line.append((zz, device(x, zz // NZL, zz % NZL, y, k)))
     me = x * NY + y
@@ -248,7 +247,7 @@
 
     def plane_sum(u):
         total = piece[u][me].astype(F32)
-        for m, _ in plane:
+        for m, _ in reversed(plane):
             arrived(plane_in[u].at[m], plane_send.at[u, m], plane_recv.at[u, m])
             total = total + plane_in[u][m].astype(F32)
         z_in[u][z] = total.astype(BF16)
@@ -290,17 +289,17 @@
     load_tiles.wait()
 
     steps = [(ch, d) for ch in range(CHUNKS) for d in range(NZL)]
-    for i in range(len(steps) + 7):
-        for lag, job in ((0, own_rows), (3, near_rows), (6, far_rows)):
+    for i in range(len(steps) + 9):
+        for lag, job in ((0, own_rows), (4, near_rows), (8, far_rows)):
             if 0 <= i - lag < len(steps):
                 job(*steps[i - lag])
-        if i == 17:
+        if i == 19:
             over_x(0)
-        if i == 21:
+        if i == 23:
             over_x(1)
             over_z(0)
-        if i >= 7:
-            multiply(*steps[i - 7])
+        if i >= 9:
+            multiply(*steps[i - 9])
     over_x(2)
     over_z(1)
     local(0)

time: 105 us -> 102 us (0.971)
  Pallas kernels: 101 us -> 97.5 us
    pallas_call x1, Pallas kernels: 101 us -> 97.5 us  [shards(): pl.pallas_call(whole_kernel, out_shape=jax.ShapeDtypeStruct((1024, 512),...]
where the time goes in v4:
time: 102 us
  Pallas kernels  97.5 us (96%)
  other arithmetic  2.81 us (3%)
  between operations  1.29 us (1%)
    pallas_call x1, Pallas kernels, shards(): pl.pallas_call(whole_kernel, out_shape=jax.ShapeDtypeStruct((1024, 512),...  97.5 us
    convert_element_type x1, other arithmetic, shards(): return (result[512:].astype(F32), result[:512].astype(F32))  2.81 us

profile of v4, /device:TPU:1, one launch (start us, length us, event | category | flops | bytes accessed | tf_op | source)
XLA Modules:
  0.0 101.6 jit_solution(8690968430213903933)
XLA Ops:
  1.3 97.5 %shard_map.95 = bf16[1024,512]{1,0:T(8,128)(2,1)} custom-call(s32[1,160]{1,0:T(1,128)} %bitcast.4, s32[1,160]{1,0:T(1,128)} %bitcast.5, s32[1,1]{1,0:T(1,128)S(6)} %copy.10.live, bf16[160,128,128]{2,1,0:T(8,128)(2,1)} %bitcast.3, bf16[128,512]{1,0:T(8,128)(2,1)} %feats_hbm.1, bf16[128,512]{1,0:T(8,128)(2,1)} %pre_hbm.1, bf16[128,512]{1,0:T(8,128)(2,1)} %cot_hbm.1, ...), custom_call_target="tpu_custom_call" | custom-call | tf_op jit(solution)/shard_map/pallas_call | solution.py:339
  98.8 2.8 %slice_convert_fusion = (f32[512,512]{1,0:T(8,128)}, f32[512,512]{1,0:T(8,128)}) fusion(bf16[1024,512]{1,0:T(8,128)(2,1)} %shard_map.95), kind=kLoop, calls=%fused_computation | loop fusion | flops 524288 | bytes 3145728 | tf_op jit(solution)/shard_map/convert_element_type | solution.py:392

commit v5 on v4

--- a/solution.py
+++ b/solution.py
@@ -185,7 +185,7 @@
 
             lax.fori_loop(0, NX, one, 0)
             return
-        for j in range(NX):
+        for j in (1, 0, 2, 3):
             q = (x + 1 + j) % NX
             value = acc[ch][q] + product(ch, base, q)
             if j < NX - 1:

time: 102 us -> 102 us (level)
  no operation moved by 1% of the time
where the time goes in v5:
time: 102 us
  Pallas kernels  97.7 us (96%)
  other arithmetic  2.81 us (3%)
  between operations  1.29 us (1%)
    pallas_call x1, Pallas kernels, shards(): pl.pallas_call(whole_kernel, out_shape=jax.ShapeDtypeStruct((1024, 512),...  97.7 us
    convert_element_type x1, other arithmetic, shards(): return (result[512:].astype(F32), result[:512].astype(F32))  2.81 us

profile of v5, /device:TPU:1, one launch (start us, length us, event | category | flops | bytes accessed | tf_op | source)
XLA Modules:
  0.0 101.8 jit_solution(5947051069846932841)
XLA Ops:
  1.3 97.7 %shard_map.95 = bf16[1024,512]{1,0:T(8,128)(2,1)} custom-call(s32[1,160]{1,0:T(1,128)} %bitcast.4, s32[1,160]{1,0:T(1,128)} %bitcast.5, s32[1,1]{1,0:T(1,128)S(6)} %copy.10.live, bf16[160,128,128]{2,1,0:T(8,128)(2,1)} %bitcast.3, bf16[128,512]{1,0:T(8,128)(2,1)} %feats_hbm.1, bf16[128,512]{1,0:T(8,128)(2,1)} %pre_hbm.1, bf16[128,512]{1,0:T(8,128)(2,1)} %cot_hbm.1, ...), custom_call_target="tpu_custom_call" | custom-call | tf_op jit(solution)/shard_map/pallas_call | solution.py:339
  99.0 2.8 %slice_convert_fusion = (f32[512,512]{1,0:T(8,128)}, f32[512,512]{1,0:T(8,128)}) fusion(bf16[1024,512]{1,0:T(8,128)(2,1)} %shard_map.95), kind=kLoop, calls=%fused_computation | loop fusion | flops 524288 | bytes 3145728 | tf_op jit(solution)/shard_map/convert_element_type | solution.py:392
